TPU v7x, 32 devices: a whole 2x2x4 slice. The times are simulated.
32 devices in a mesh: win: 8 (over z, y), seq: 4 (over x, core).
Axes of the slice: x: 2, y: 2, z: 4, core: 2. Of those that a mesh axis runs over, the one named last changes fastest.
Arguments:
- queries: bfloat16 [2, 8, 2048, 2048], P(None, 'win', 'seq'), may hold values from -4.5 to 4.5
- key_states: bfloat16 [2, 8, 2048, 2048], P(None, 'win', 'seq'), may hold values from -4.5 to 4.5
- value_states: bfloat16 [2, 8, 2048, 2048], P(None, 'win', 'seq'), may hold values from -5 to 5
- out_grad: bfloat16 [2, 8, 2048, 2048], P(None, 'win', 'seq'), may hold values from -60 to 60
Outputs:
- query_grad: bfloat16 [2, 8, 2048, 2048], P(None, 'win', 'seq')
- key_grad: bfloat16 [2, 8, 2048, 2048], P(None, 'win', 'seq')
- value_grad: bfloat16 [2, 8, 2048, 2048], P(None, 'win', 'seq')
All inputs are finite; a program needn't handle non-finite values.
Results may differ from a plain program's by a relative error of at most 0.0095.
Values may be sent and summed in bfloat16 or wider, within the bound.
No kernel may reach another device: no remote copies, remote signals or barrier semaphores. Data moves between devices by JAX's collectives and lax.ppermute only.
A program may use at most 192 MiB of HBM per device.

v0:
```python
import jax
import jax.numpy as jnp
from jax import lax
from jax.sharding import PartitionSpec as P

HEADS = 16
HDIM = 128
ROWS = 32
COLS = 64


def passed_along(block, axis, distance):
    devices = range(lax.axis_size(axis))
    route = [((i - distance) % len(devices), i) for i in devices]
    return lax.ppermute(block, axis, route)


def ahead_columns(values, col_axis):
    middle = values.shape[col_axis] // 2
    arrived = passed_along(lax.slice_in_dim(values, 0, middle, axis=col_axis), "win", -1)
    return jnp.concatenate(
        [lax.slice_in_dim(values, middle, 2 * middle, axis=col_axis), arrived], axis=col_axis
    )


def behind_columns(values, col_axis):
    middle = values.shape[col_axis] // 2
    arrived = passed_along(lax.slice_in_dim(values, middle, 2 * middle, axis=col_axis), "win", 1)
    return jnp.concatenate(
        [arrived, lax.slice_in_dim(values, 0, middle, axis=col_axis)], axis=col_axis
    )


def back_to_tokens(gradients):
    return lax.all_to_all(gradients, "seq", split_axis=2, concat_axis=3, tiled=True)


def window_grads(query_heads, key_heads, value_heads, grad_heads):
    samples_here, tokens, own_heads, head_size = query_heads.shape
    block_rows = min(512, tokens)
    factor = head_size ** (-0.5)

    def one_block(totals, offset):
        key_total, value_total = totals
        query_block = lax.dynamic_slice_in_dim(query_heads, offset, block_rows, 1)
        grad_block = lax.dynamic_slice_in_dim(grad_heads, offset, block_rows, 1)
        scores = (
            jnp.einsum(
                "bqhd,bkhd->bhqk", query_block, key_heads, preferred_element_type=jnp.float32
            )
            * factor
        )
        scores = scores - jnp.max(scores, axis=3, keepdims=True)
        weights = jnp.exp(scores)
        weights = weights / jnp.sum(weights, axis=3, keepdims=True)
        weights_low = weights.astype(jnp.bfloat16)
        value_total = value_total + jnp.einsum(
            "bhqk,bqhd->bkhd", weights_low, grad_block, preferred_element_type=jnp.float32
        )
        grad_probs = jnp.einsum(
            "bqhd,bkhd->bhqk", grad_block, value_heads, preferred_element_type=jnp.float32
        )
        row_dot = jnp.sum(weights * grad_probs, axis=3, keepdims=True)
        grad_scores = (weights * (grad_probs - row_dot) * factor).astype(jnp.bfloat16)
        query_block_grad = jnp.einsum(
            "bhqk,bkhd->bqhd", grad_scores, key_heads, preferred_element_type=jnp.float32
        ).astype(jnp.bfloat16)
        key_total = key_total + jnp.einsum(
            "bhqk,bqhd->bkhd", grad_scores, query_block, preferred_element_type=jnp.float32
        )
        return ((key_total, value_total), query_block_grad)

    starts = jnp.arange(tokens // block_rows, dtype=jnp.int32) * block_rows
    zero_acc = jnp.zeros(query_heads.shape, jnp.float32)
    (key_total, value_total), query_blocks = lax.scan(one_block, (zero_acc, zero_acc), starts)
    query_grad = jnp.moveaxis(query_blocks, 0, 1).reshape(
        samples_here, tokens, own_heads, head_size
    )
    return jnp.stack([query_grad, key_total.astype(jnp.bfloat16), value_total.astype(jnp.bfloat16)])


def on_device(queries, key_states, value_states, out_grad):
    samples = queries.shape[0]
    local_tokens = queries.shape[2]
    model_width = queries.shape[3]

    def head_view(values):
        return values.reshape(samples, local_tokens, HEADS, HDIM)

    sent_grad = head_view(out_grad)
    query_heads = lax.all_to_all(head_view(queries), "seq", split_axis=2, concat_axis=1, tiled=True)
    key_heads = lax.all_to_all(
        head_view(key_states), "seq", split_axis=2, concat_axis=1, tiled=True
    )
    value_heads = lax.all_to_all(
        head_view(value_states), "seq", split_axis=2, concat_axis=1, tiled=True
    )
    grad_heads = lax.all_to_all(sent_grad, "seq", split_axis=2, concat_axis=1, tiled=True)
    item_count, tokens, own_heads, head_size = query_heads.shape
    head_grid = grad_heads.reshape(item_count, ROWS, COLS, own_heads, head_size)
    head_grid = jnp.roll(ahead_columns(head_grid, 2), -(ROWS // 2), axis=1)
    grad_heads = head_grid.reshape(item_count, tokens, own_heads, head_size)
    gradients = window_grads(query_heads, key_heads, value_heads, grad_heads)
    back_grid = gradients.reshape(3, item_count, ROWS, COLS, own_heads, head_size)
    back_grid = behind_columns(jnp.roll(back_grid, ROWS // 2, axis=2), 3)
    gradients = back_grid.reshape(3, item_count, tokens, own_heads, head_size)
    result = gradients
    result = back_to_tokens(result)
    pieces = result.reshape(3, samples, 1, local_tokens, model_width)
    return (pieces[0], pieces[1], pieces[2])


def solution(mesh):
    placed = (
        P(None, "win", "seq", None),
        P(None, "win", "seq", None),
        P(None, "win", "seq", None),
        P(None, "win", "seq", None),
    )
    return jax.shard_map(
        on_device,
        mesh=mesh,
        in_specs=placed,
        out_specs=(
            P(None, "win", "seq", None),
            P(None, "win", "seq", None),
            P(None, "win", "seq", None),
        ),
        check_vma=False,
    )
```

profile of v0, /device:TPU:0, one launch (start us, length us, event | category | flops | bytes accessed | tf_op | source)
XLA Modules:
  0.0 1256.4 jit_solution(8506165742562413556)
XLA Ops:
  0.6 6.2 copy.91
  6.8 4.6 copy.92
  11.5 4.8 all-to-all-start
  16.3 6.2 copy.95
  22.5 4.6 copy.96
  27.2 38.0 %all-to-all-done = bf16[2,512,16,128]{1,3,0,2:T(8,128)(2,1)} async-done(((bf16[2,512,16,128]{1,3,0,2:T(8,128)(2,1)}), bf16[2,512,16,128]{1,3,0,2:T(8,128)(2,1)}, u32[]{:S(2)}, u32[]{:S(2)}) %all-to-all-start) | async-done | bytes 4194336 | tf_op jit(solution)/shard_map/all_to_all | solution.py:91
  65.2 4.8 all-to-all-start.1
  70.1 6.2 copy.99
  76.3 6.4 copy.100
  82.7 35.6 %all-to-all-done.1 = bf16[2,512,16,128]{1,3,0,2:T(8,128)(2,1)} async-done(((bf16[2,512,16,128]{1,3,0,2:T(8,128)(2,1)}), bf16[2,512,16,128]{1,3,0,2:T(8,128)(2,1)}, u32[]{:S(2)}, u32[]{:S(2)}) %all-to-all-start.1) | async-done | bytes 4194336 | tf_op jit(solution)/shard_map/all_to_all | solution.py:92
  118.3 4.8 all-to-all-start.2
  123.1 6.2 copy.103
  129.3 4.6 copy.104
  133.9 37.4 %all-to-all-done.2 = bf16[2,512,16,128]{3,1,0,2:T(8,128)(2,1)} async-done(((bf16[2,512,16,128]{3,1,0,2:T(8,128)(2,1)}), bf16[2,512,16,128]{3,1,0,2:T(8,128)(2,1)}, u32[]{:S(2)}, u32[]{:S(2)}) %all-to-all-start.2) | async-done | bytes 4194336 | tf_op jit(solution)/shard_map/all_to_all | solution.py:98
  171.3 4.9 all-to-all-start.3
  176.2 2.5 copy.102
  178.7 2.4 fusion.82
  181.1 5.4 collective-permute-start
  186.5 7.2 copy.94
  193.7 7.2 copy.98
  201.0 23.5 %all-to-all-done.3 = bf16[2,512,16,128]{1,3,0,2:T(8,128)(2,1)} async-done(((bf16[2,512,16,128]{1,3,0,2:T(8,128)(2,1)}), bf16[2,512,16,128]{1,3,0,2:T(8,128)(2,1)}, u32[]{:S(2)}, u32[]{:S(2)}) %all-to-all-start.3) | async-done | bytes 4194336 | tf_op jit(solution)/shard_map/all_to_all | solution.py:95
  224.4 7.3 copy.106
  232.3 1.5 fusion.74
  233.8 3.2 fusion.73
  237.0 600.8 %while.15 = (s32[]{:T(128)}, f32[2,2048,4,128]{1,3,2,0:T(8,128)}, f32[2,2048,4,128]{1,3,2,0:T(8,128)}, bf16[4,2,512,4,128]{4,2,0,3,1:T(8,128)(2,1)}, s32[4]{0:T(...) while((s32[]{:T(128)}, f32[2,2048,4,128]{1,3,2,0:T(8,128)}, ...), condition=%wide.region_4.5_spmd.clone, body=%wide.region_0.4_spmd.clone.sunk | while | flops 13069996032 | bytes 392267616 | solution.py:75
  239.6 18.1 %fusion.118 = f32[2,4,512,2048]{3,2,1,0:T(8,128)} fusion(bf16[2,2048,4,128]{3,1,2,0:T(8,128)(2,1)} %get-tuple-element.215, bf16[2,2048,4,128]{3,1,2,0:T(8,128)(2,1)} %get-tuple-element.214, s32[]{:T(128)S(6)} %select_n.6), kind=kOutput, calls=%fused_computation.21.clone.1 | convolution fusion | flops 2147483648 | bytes 38797316 | tf_op jit(solution)/shard_map/while/body/eval_jaxpr/bqhd,bkhd->bhqk/dot_general | solution.py:60
  257.7 17.5 %fusion.119 = (f32[2,4,512]{2,1,0:T(4,128)S(1)}, f32[2,4,512,2048]{3,2,1,0:T(8,128)}) fusion(bf16[2,2048,4,128]{3,1,2,0:T(8,128)(2,1)} %get-tuple-element.213, bf16[2,2048,4,128]{3,1,2,0:T(8,128)(2,1)} %get-tuple-element.212, s32[]{:T(128)S(6)} %select_n.6), kind=kOutput, calls=%fused_computation.49.clone.1 | convolution fusion | flops 2172651520 | bytes 38813700 | tf_op jit(solution)/shard_map/while/body/eval_jaxpr/sub | solution.py:53
  275.3 45.7 %fusion.120 = bf16[4,2,512,4,128]{4,2,0,3,1:T(8,128)(2,1)} fusion(bf16[4,2,512,4,128]{4,2,0,3,1:T(8,128)(2,1)} %get-tuple-element.198, s32[]{:T(128)S(6)} %copy.131, bf16[2,2048,4,128]{3,1,2,0:T(8,128)(2,1)} %get-tuple-element.213, f32[2,4,512,2048]{3,2,1,0:T(8,128)} %fusion.118, f32[2,4,512,2048]{3,2,1,0:T(8,128)} %get-tuple-element.181, ...), kind=kOutput, calls=%fused_computation.19.clone.1 | convolution fusion | flops 2206734336 | bytes 139493376 | tf_op jit(solution)/shard_map/while/body/eval_jaxpr/bhqk,bkhd->bqhd/dot_general | solution.py:65
  321.0 46.5 %bitcast_add_fusion.4 = f32[2,2048,4,128]{1,3,2,0:T(8,128)} fusion(f32[2,2048,4,128]{1,3,2,0:T(8,128)} %get-tuple-element.196, f32[2,4,512,2048]{3,2,1,0:T(8,128)} %fusion.118, pred[]{:T(512)S(6)} %compare.3, bf16[2,2048,4,128]{3,1,2,0:T(8,128)(2,1)} %get-tuple-element.212, s32[]{:T(128)S(6)} %select_n.6, ...), kind=kOutput, calls=%fused_computation.16.clone.1 | convolution fusion | flops 2210404352 | bytes 152076288 | tf_op jit(solution)/shard_map/while/body/eval_jaxpr/bhqk,bqhd->bkhd/dot_general | solution.py:68
  367.4 17.1 %bitcast_add_fusion.5 = f32[2,2048,4,128]{1,3,2,0:T(8,128)} fusion(f32[2,2048,4,128]{1,3,2,0:T(8,128)} %get-tuple-element.197, pred[]{:T(512)S(6)} %compare.3, bf16[2,2048,4,128]{3,1,2,0:T(8,128)(2,1)} %get-tuple-element.214, s32[]{:T(128)S(6)} %select_n.6, f32[2,4,512]{2,1,0:T(4,128)S(1)} %get-tuple-element.182, ...), kind=kOutput, calls=%fused_computation.15.clone.1 | convolution fusion | flops 4332722176 | bytes 23086592 | tf_op jit(solution)/shard_map/while/body/eval_jaxpr/bhqk,bqhd->bkhd/dot_general | solution.py:57
  387.1 18.1 %fusion.118 = f32[2,4,512,2048]{3,2,1,0:T(8,128)} fusion(bf16[2,2048,4,128]{3,1,2,0:T(8,128)(2,1)} %get-tuple-element.215, bf16[2,2048,4,128]{3,1,2,0:T(8,128)(2,1)} %get-tuple-element.214, s32[]{:T(128)S(6)} %select_n.6), kind=kOutput, calls=%fused_computation.21.clone.1 | convolution fusion | flops 2147483648 | bytes 38797316 | tf_op jit(solution)/shard_map/while/body/eval_jaxpr/bqhd,bkhd->bhqk/dot_general | solution.py:60
  405.2 17.5 %fusion.119 = (f32[2,4,512]{2,1,0:T(4,128)S(1)}, f32[2,4,512,2048]{3,2,1,0:T(8,128)}) fusion(bf16[2,2048,4,128]{3,1,2,0:T(8,128)(2,1)} %get-tuple-element.213, bf16[2,2048,4,128]{3,1,2,0:T(8,128)(2,1)} %get-tuple-element.212, s32[]{:T(128)S(6)} %select_n.6), kind=kOutput, calls=%fused_computation.49.clone.1 | convolution fusion | flops 2172651520 | bytes 38813700 | tf_op jit(solution)/shard_map/while/body/eval_jaxpr/sub | solution.py:53
  422.8 45.7 %fusion.120 = bf16[4,2,512,4,128]{4,2,0,3,1:T(8,128)(2,1)} fusion(bf16[4,2,512,4,128]{4,2,0,3,1:T(8,128)(2,1)} %get-tuple-element.198, s32[]{:T(128)S(6)} %copy.131, bf16[2,2048,4,128]{3,1,2,0:T(8,128)(2,1)} %get-tuple-element.213, f32[2,4,512,2048]{3,2,1,0:T(8,128)} %fusion.118, f32[2,4,512,2048]{3,2,1,0:T(8,128)} %get-tuple-element.181, ...), kind=kOutput, calls=%fused_computation.19.clone.1 | convolution fusion | flops 2206734336 | bytes 139493376 | tf_op jit(solution)/shard_map/while/body/eval_jaxpr/bhqk,bkhd->bqhd/dot_general | solution.py:65
  468.5 48.8 %bitcast_add_fusion.4 = f32[2,2048,4,128]{1,3,2,0:T(8,128)} fusion(f32[2,2048,4,128]{1,3,2,0:T(8,128)} %get-tuple-element.196, f32[2,4,512,2048]{3,2,1,0:T(8,128)} %fusion.118, pred[]{:T(512)S(6)} %compare.3, bf16[2,2048,4,128]{3,1,2,0:T(8,128)(2,1)} %get-tuple-element.212, s32[]{:T(128)S(6)} %select_n.6, ...), kind=kOutput, calls=%fused_computation.16.clone.1 | convolution fusion | flops 2210404352 | bytes 152076288 | tf_op jit(solution)/shard_map/while/body/eval_jaxpr/bhqk,bqhd->bkhd/dot_general | solution.py:68
  517.3 18.4 %bitcast_add_fusion.5 = f32[2,2048,4,128]{1,3,2,0:T(8,128)} fusion(f32[2,2048,4,128]{1,3,2,0:T(8,128)} %get-tuple-element.197, pred[]{:T(512)S(6)} %compare.3, bf16[2,2048,4,128]{3,1,2,0:T(8,128)(2,1)} %get-tuple-element.214, s32[]{:T(128)S(6)} %select_n.6, f32[2,4,512]{2,1,0:T(4,128)S(1)} %get-tuple-element.182, ...), kind=kOutput, calls=%fused_computation.15.clone.1 | convolution fusion | flops 4332722176 | bytes 23086592 | tf_op jit(solution)/shard_map/while/body/eval_jaxpr/bhqk,bqhd->bkhd/dot_general | solution.py:57
  535.7 0.7 dynamic_slice.50
  538.2 18.1 %fusion.118 = f32[2,4,512,2048]{3,2,1,0:T(8,128)} fusion(bf16[2,2048,4,128]{3,1,2,0:T(8,128)(2,1)} %get-tuple-element.215, bf16[2,2048,4,128]{3,1,2,0:T(8,128)(2,1)} %get-tuple-element.214, s32[]{:T(128)S(6)} %select_n.6), kind=kOutput, calls=%fused_computation.21.clone.1 | convolution fusion | flops 2147483648 | bytes 38797316 | tf_op jit(solution)/shard_map/while/body/eval_jaxpr/bqhd,bkhd->bhqk/dot_general | solution.py:60
  556.4 17.5 %fusion.119 = (f32[2,4,512]{2,1,0:T(4,128)S(1)}, f32[2,4,512,2048]{3,2,1,0:T(8,128)}) fusion(bf16[2,2048,4,128]{3,1,2,0:T(8,128)(2,1)} %get-tuple-element.213, bf16[2,2048,4,128]{3,1,2,0:T(8,128)(2,1)} %get-tuple-element.212, s32[]{:T(128)S(6)} %select_n.6), kind=kOutput, calls=%fused_computation.49.clone.1 | convolution fusion | flops 2172651520 | bytes 38813700 | tf_op jit(solution)/shard_map/while/body/eval_jaxpr/sub | solution.py:53
  573.9 45.7 %fusion.120 = bf16[4,2,512,4,128]{4,2,0,3,1:T(8,128)(2,1)} fusion(bf16[4,2,512,4,128]{4,2,0,3,1:T(8,128)(2,1)} %get-tuple-element.198, s32[]{:T(128)S(6)} %copy.131, bf16[2,2048,4,128]{3,1,2,0:T(8,128)(2,1)} %get-tuple-element.213, f32[2,4,512,2048]{3,2,1,0:T(8,128)} %fusion.118, f32[2,4,512,2048]{3,2,1,0:T(8,128)} %get-tuple-element.181, ...), kind=kOutput, calls=%fused_computation.19.clone.1 | convolution fusion | flops 2206734336 | bytes 139493376 | tf_op jit(solution)/shard_map/while/body/eval_jaxpr/bhqk,bkhd->bqhd/dot_general | solution.py:65
  619.6 48.8 %bitcast_add_fusion.4 = f32[2,2048,4,128]{1,3,2,0:T(8,128)} fusion(f32[2,2048,4,128]{1,3,2,0:T(8,128)} %get-tuple-element.196, f32[2,4,512,2048]{3,2,1,0:T(8,128)} %fusion.118, pred[]{:T(512)S(6)} %compare.3, bf16[2,2048,4,128]{3,1,2,0:T(8,128)(2,1)} %get-tuple-element.212, s32[]{:T(128)S(6)} %select_n.6, ...), kind=kOutput, calls=%fused_computation.16.clone.1 | convolution fusion | flops 2210404352 | bytes 152076288 | tf_op jit(solution)/shard_map/while/body/eval_jaxpr/bhqk,bqhd->bkhd/dot_general | solution.py:68
  668.4 18.4 %bitcast_add_fusion.5 = f32[2,2048,4,128]{1,3,2,0:T(8,128)} fusion(f32[2,2048,4,128]{1,3,2,0:T(8,128)} %get-tuple-element.197, pred[]{:T(512)S(6)} %compare.3, bf16[2,2048,4,128]{3,1,2,0:T(8,128)(2,1)} %get-tuple-element.214, s32[]{:T(128)S(6)} %select_n.6, f32[2,4,512]{2,1,0:T(4,128)S(1)} %get-tuple-element.182, ...), kind=kOutput, calls=%fused_computation.15.clone.1 | convolution fusion | flops 4332722176 | bytes 23086592 | tf_op jit(solution)/shard_map/while/body/eval_jaxpr/bhqk,bqhd->bkhd/dot_general | solution.py:57
  689.3 18.1 %fusion.118 = f32[2,4,512,2048]{3,2,1,0:T(8,128)} fusion(bf16[2,2048,4,128]{3,1,2,0:T(8,128)(2,1)} %get-tuple-element.215, bf16[2,2048,4,128]{3,1,2,0:T(8,128)(2,1)} %get-tuple-element.214, s32[]{:T(128)S(6)} %select_n.6), kind=kOutput, calls=%fused_computation.21.clone.1 | convolution fusion | flops 2147483648 | bytes 38797316 | tf_op jit(solution)/shard_map/while/body/eval_jaxpr/bqhd,bkhd->bhqk/dot_general | solution.py:60
  707.5 17.5 %fusion.119 = (f32[2,4,512]{2,1,0:T(4,128)S(1)}, f32[2,4,512,2048]{3,2,1,0:T(8,128)}) fusion(bf16[2,2048,4,128]{3,1,2,0:T(8,128)(2,1)} %get-tuple-element.213, bf16[2,2048,4,128]{3,1,2,0:T(8,128)(2,1)} %get-tuple-element.212, s32[]{:T(128)S(6)} %select_n.6), kind=kOutput, calls=%fused_computation.49.clone.1 | convolution fusion | flops 2172651520 | bytes 38813700 | tf_op jit(solution)/shard_map/while/body/eval_jaxpr/sub | solution.py:53
  725.0 45.7 %fusion.120 = bf16[4,2,512,4,128]{4,2,0,3,1:T(8,128)(2,1)} fusion(bf16[4,2,512,4,128]{4,2,0,3,1:T(8,128)(2,1)} %get-tuple-element.198, s32[]{:T(128)S(6)} %copy.131, bf16[2,2048,4,128]{3,1,2,0:T(8,128)(2,1)} %get-tuple-element.213, f32[2,4,512,2048]{3,2,1,0:T(8,128)} %fusion.118, f32[2,4,512,2048]{3,2,1,0:T(8,128)} %get-tuple-element.181, ...), kind=kOutput, calls=%fused_computation.19.clone.1 | convolution fusion | flops 2206734336 | bytes 139493376 | tf_op jit(solution)/shard_map/while/body/eval_jaxpr/bhqk,bkhd->bqhd/dot_general | solution.py:65
  770.7 48.8 %bitcast_add_fusion.4 = f32[2,2048,4,128]{1,3,2,0:T(8,128)} fusion(f32[2,2048,4,128]{1,3,2,0:T(8,128)} %get-tuple-element.196, f32[2,4,512,2048]{3,2,1,0:T(8,128)} %fusion.118, pred[]{:T(512)S(6)} %compare.3, bf16[2,2048,4,128]{3,1,2,0:T(8,128)(2,1)} %get-tuple-element.212, s32[]{:T(128)S(6)} %select_n.6, ...), kind=kOutput, calls=%fused_computation.16.clone.1 | convolution fusion | flops 2210404352 | bytes 152076288 | tf_op jit(solution)/shard_map/while/body/eval_jaxpr/bhqk,bqhd->bkhd/dot_general | solution.py:68
  819.5 18.4 %bitcast_add_fusion.5 = f32[2,2048,4,128]{1,3,2,0:T(8,128)} fusion(f32[2,2048,4,128]{1,3,2,0:T(8,128)} %get-tuple-element.197, pred[]{:T(512)S(6)} %compare.3, bf16[2,2048,4,128]{3,1,2,0:T(8,128)(2,1)} %get-tuple-element.214, s32[]{:T(128)S(6)} %select_n.6, f32[2,4,512]{2,1,0:T(4,128)S(1)} %get-tuple-element.182, ...), kind=kOutput, calls=%fused_computation.15.clone.1 | convolution fusion | flops 4332722176 | bytes 23086592 | tf_op jit(solution)/shard_map/while/body/eval_jaxpr/bhqk,bqhd->bkhd/dot_general | solution.py:57
  837.9 7.1 copy.108
  845.0 7.1 copy.109
  852.1 6.4 pad_maximum_fusion.1
  858.5 4.0 fusion.81
  862.5 0.7 fusion.72
  863.2 1.8 collective-permute-start.1
  865.0 138.7 %collective-permute-done.1 = bf16[3,2,32,32,4,128]{5,3,2,4,1,0:T(8,128)(2,1)S(1)} collective-permute-done((bf16[3,2,32,32,4,128]{5,3,2,4,1,0:T(8,128)(2,1)S(1)}, bf16[3,2,32,32,4,128]{5,3,2,4,1,0:T(8,128)(2,1)S(1)}, u32[]{:S(2)}, u32[]{:S(2)}) %collective-permute-start.1) | collective-permute-done | bytes 6291488 | tf_op jit(solution)/shard_map/ppermute | solution.py:15
  1003.7 1.6 fusion.71
  1005.3 50.2 %copy.110 = bf16[3,2,2048,4,128]{4,3,1,0,2:T(4,128)(2,1)S(1)} copy(bf16[3,2,2048,4,128]{4,2,3,1,0:T(8,128)(2,1)S(1)} %bitcast.70) | data formatting | bytes 25165824 | tf_op jit(solution)/shard_map/reshape | solution.py:106
  1055.6 141.0 %all_to_all.84 = bf16[3,2,2048,4,128]{4,3,1,0,2:T(4,128)(2,1)S(1)} all-to-all(bf16[3,2,2048,4,128]{4,3,1,0,2:T(4,128)(2,1)S(1)} %copy.110), channel_id=1, replica_groups=mesh['win'=8,'seq'=4] {'seq'}, dimensions={2} | all-to-all | bytes 25165824 | tf_op jit(solution)/shard_map/all_to_all | solution.py:35
  1196.5 14.8 %copy.111 = bf16[3,2,2048,4,128]{4,2,3,1,0:T(8,128)(2,1)S(1)} copy(bf16[3,2,2048,4,128]{4,3,1,0,2:T(4,128)(2,1)S(1)} %all_to_all.84) | data formatting | bytes 25165824 | tf_op jit(solution)/shard_map/all_to_all | solution.py:35
  1211.3 4.8 fusion.80
  1216.1 7.3 copy.114
  1223.4 6.2 copy.117
  1229.6 7.3 copy.113
  1236.8 6.2 copy.116
  1243.0 7.3 copy.112
  1250.2 6.2 copy.115
  (24 shorter events, 2.6 us)
Async XLA Ops:
  11.5 53.7 %all-to-all-start = ((bf16[2,512,16,128]{1,3,0,2:T(8,128)(2,1)}), bf16[2,512,16,128]{1,3,0,2:T(8,128)(2,1)}, u32[]{:S(2)}, u32[]{:S(2)}) async-start(bf16[2,512,16,128]{1,3,0,2:T(8,128)(2,1)} %copy.92), calls=%async_computation | async-start | bytes 8388608 | tf_op jit(solution)/shard_map/all_to_all | solution.py:91
  65.2 53.1 %all-to-all-start.1 = ((bf16[2,512,16,128]{1,3,0,2:T(8,128)(2,1)}), bf16[2,512,16,128]{1,3,0,2:T(8,128)(2,1)}, u32[]{:S(2)}, u32[]{:S(2)}) async-start(bf16[2,512,16,128]{1,3,0,2:T(8,128)(2,1)} %copy.96), calls=%async_computation.1 | async-start | bytes 8388608 | tf_op jit(solution)/shard_map/all_to_all | solution.py:92
  118.3 53.1 %all-to-all-start.2 = ((bf16[2,512,16,128]{3,1,0,2:T(8,128)(2,1)}), bf16[2,512,16,128]{3,1,0,2:T(8,128)(2,1)}, u32[]{:S(2)}, u32[]{:S(2)}) async-start(bf16[2,512,16,128]{3,1,0,2:T(8,128)(2,1)} %copy.100), calls=%async_computation.2 | async-start | bytes 8388608 | tf_op jit(solution)/shard_map/all_to_all | solution.py:98
  171.3 53.1 %all-to-all-start.3 = ((bf16[2,512,16,128]{1,3,0,2:T(8,128)(2,1)}), bf16[2,512,16,128]{1,3,0,2:T(8,128)(2,1)}, u32[]{:S(2)}, u32[]{:S(2)}) async-start(bf16[2,512,16,128]{1,3,0,2:T(8,128)(2,1)} %copy.104), calls=%async_computation.3 | async-start | bytes 8388608 | tf_op jit(solution)/shard_map/all_to_all | solution.py:95
  181.1 51.2 %collective-permute-start = (bf16[2,32,32,4,128]{4,2,1,3,0:T(8,128)(2,1)}, bf16[2,32,32,4,128]{4,2,1,3,0:T(8,128)(2,1)}, u32[]{:S(2)}, u32[]{:S(2)}) collective-permute-start(bf16[2,32,32,4,128]{4,2,1,3,0:T(8,128)(2,1)} %get-tuple-element.123), channel_id=1, source_target_pairs={{4,0},{8,4},{12,8},{16,12},{20,16},{24,20},{28,24},{0,28},{5,1},{9... | collective-permute-start | bytes 6291464 | tf_op jit(solution)/shard_map/ppermute | solution.py:15
  237.0 20.7 %copy-start = (s32[4]{0:T(128)}, s32[4]{0:T(128)S(1)}, u32[]{:S(2)}) copy-start(s32[4]{0:T(128)S(1)} %get-tuple-element.211) | copy-start | bytes 52 | tf_op jit(solution)/shard_map/while
  367.4 17.1 %copy-start.1 = (s32[4]{0:T(128)S(1)}, s32[4]{0:T(128)}, u32[]{:S(2)}) copy-start(s32[4]{0:T(128)} %copy-done) | copy-start | bytes 52 | tf_op jit(solution)/shard_map/while
  384.5 20.7 %copy-start = (s32[4]{0:T(128)}, s32[4]{0:T(128)S(1)}, u32[]{:S(2)}) copy-start(s32[4]{0:T(128)S(1)} %get-tuple-element.211) | copy-start | bytes 52 | tf_op jit(solution)/shard_map/while
  517.3 18.4 %copy-start.1 = (s32[4]{0:T(128)S(1)}, s32[4]{0:T(128)}, u32[]{:S(2)}) copy-start(s32[4]{0:T(128)} %copy-done) | copy-start | bytes 52 | tf_op jit(solution)/shard_map/while
  535.7 20.7 %copy-start = (s32[4]{0:T(128)}, s32[4]{0:T(128)S(1)}, u32[]{:S(2)}) copy-start(s32[4]{0:T(128)S(1)} %get-tuple-element.211) | copy-start | bytes 52 | tf_op jit(solution)/shard_map/while
  668.4 18.4 %copy-start.1 = (s32[4]{0:T(128)S(1)}, s32[4]{0:T(128)}, u32[]{:S(2)}) copy-start(s32[4]{0:T(128)} %copy-done) | copy-start | bytes 52 | tf_op jit(solution)/shard_map/while
  686.8 20.7 %copy-start = (s32[4]{0:T(128)}, s32[4]{0:T(128)S(1)}, u32[]{:S(2)}) copy-start(s32[4]{0:T(128)S(1)} %get-tuple-element.211) | copy-start | bytes 52 | tf_op jit(solution)/shard_map/while
  819.5 18.4 %copy-start.1 = (s32[4]{0:T(128)S(1)}, s32[4]{0:T(128)}, u32[]{:S(2)}) copy-start(s32[4]{0:T(128)} %copy-done) | copy-start | bytes 52 | tf_op jit(solution)/shard_map/while
  863.2 140.5 %collective-permute-start.1 = (bf16[3,2,32,32,4,128]{5,3,2,4,1,0:T(8,128)(2,1)S(1)}, bf16[3,2,32,32,4,128]{5,3,2,4,1,0:T(8,128)(2,1)S(1)}, u32[]{:S(2)}, u32[]{:S(2)}) collective-permute-start(bf16[3,2,32,32,4,128]{5,3,2,4,1,0:T(8,128)(2,1)S(1)} %fusion.72), channel_id=1, source_target_pairs={{28,0},{0,4},{4,8},{8,12},{12,16},{16,20},{20,24},{24,28},{29,1},{... | collective-permute-start | bytes 18874376 | tf_op jit(solution)/shard_map/ppermute | solution.py:15
where the time goes:
time: 1260 us
  matrix products  591 us (47%)
  waiting for transfers between devices  274 us (22%)
  local copies, waits for them, and re-layouts  203 us (16%)
  blocking collectives  141 us (11%)
  starting transfers between devices  26.6 us (2%)
  other arithmetic  13.4 us (1%)
    dot_general x4, matrix products, one_block(): jnp.einsum('bhqk,bqhd->bkhd', grad_scores, query_block, preferred_element...  193 us
    dot_general x4, matrix products, one_block(): jnp.einsum('bhqk,bkhd->bqhd', grad_scores, key_heads, preferred_element_t...  183 us
    all_to_all x1, blocking collectives, back_to_tokens(): lax.all_to_all(gradients, 'seq', split_axis=2, concat_axis=3, tiled=True)  141 us
    ppermute x2, waiting for transfers between devices, passed_along(): return lax.ppermute(block, axis, route)  139 us
    dot_general x4, matrix products, one_block(): jnp.einsum('bqhd,bkhd->bhqk', grad_block, value_heads, preferred_element_...  72.5 us
    dot_general x4, matrix products, one_block(): jnp.einsum('bhqk,bqhd->bkhd', weights_low, grad_block, preferred_element_...  72.2 us
    sub x4, matrix products, one_block(): scores = scores - jnp.max(scores, axis=3, keepdims=True)  70.1 us
    reshape x1, local copies, waits for them, and re-layouts, on_device(): gradients = back_grid.reshape(3, item_count, tokens, own_heads, head_size)  50.2 us
  transfers between devices with their start and end apart: 6, of which 6 were waited for; matrix products, arithmetic and copies ran while one was open for 5% of the time, Pallas kernels for 0%

commit v1 on v0

--- a/solution.py
+++ b/solution.py
@@ -1,3 +1,4 @@
+import functools
 import jax
 import jax.numpy as jnp
 from jax import lax
@@ -7,6 +8,17 @@
 HDIM = 128
 ROWS = 32
 COLS = 64
+
+
+def _proceed_block(incoming_x, shard_axis):
+    big = lax.all_to_all(
+        jnp.stack(jnp.split(incoming_x, lax.axis_size(shard_axis), 2)), shard_axis, 0, 0
+    )
+    t_next = jnp.concatenate(big, 3)
+    return t_next
+
+
+rows_cover = functools.partial(_proceed_block, shard_axis="seq")
 
 
 def passed_along(block, axis, distance):
@@ -32,7 +44,7 @@
 
 
 def back_to_tokens(gradients):
-    return lax.all_to_all(gradients, "seq", split_axis=2, concat_axis=3, tiled=True)
+    return rows_cover(gradients)
 
 
 def window_grads(query_heads, key_heads, value_heads, grad_heads):

time: 1260 us -> 1220 us (0.968)
  local copies, waits for them, and re-layouts: 203 us -> 141 us
  loops' own time: 7.64 us -> 22.1 us
    reshape x1 -> x0, local copies, waits for them, and re-layouts: 50.2 us -> none  [on_device(): gradients = back_grid.reshape(3, item_count, tokens, own_heads, head_size)]
    squeeze x0 -> x3, local copies, waits for them, and re-layouts: none -> 23.3 us  [on_device(): return (pieces[0], pieces[1], pieces[2])]
    unnamed x7 -> x4, local copies, waits for them, and re-layouts: 43.4 us -> 24.9 us
    all_to_all x1 -> x0, local copies, waits for them, and re-layouts: 14.8 us -> none  [back_to_tokens(): lax.all_to_all(gradients, 'seq', split_axis=2, concat_axis=3, tiled=True)]
    another operation x1, loops' own time: 7.64 us -> 22.1 us  [window_grads(): lax.scan(one_block, (zero_acc, zero_acc), starts)]
where the time goes in v1:
time: 1220 us; the launch traced here: 1210 us
  matrix products  591 us (48%)
  waiting for transfers between devices  274 us (22%)
  local copies, waits for them, and re-layouts  141 us (12%)
  blocking collectives  141 us (12%)
  starting transfers between devices  26.6 us (2%)
  loops' own time  22.1 us (2%)
  other arithmetic  15.1 us (1%)
    dot_general x4, matrix products, one_block(): jnp.einsum('bhqk,bqhd->bkhd', grad_scores, query_block, preferred_element...  193 us
    dot_general x4, matrix products, one_block(): jnp.einsum('bhqk,bkhd->bqhd', grad_scores, key_heads, preferred_element_t...  183 us
    all_to_all x1, blocking collectives, _proceed_block(): lax.all_to_all(jnp.stack(jnp.split(incoming_x, lax.axis_size(shard_axis),...  141 us
    ppermute x2, waiting for transfers between devices, passed_along(): return lax.ppermute(block, axis, route)  139 us
    dot_general x4, matrix products, one_block(): jnp.einsum('bqhd,bkhd->bhqk', grad_block, value_heads, preferred_element_...  72.5 us
    dot_general x4, matrix products, one_block(): jnp.einsum('bhqk,bqhd->bkhd', weights_low, grad_block, preferred_element_...  72.1 us
    sub x4, matrix products, one_block(): scores = scores - jnp.max(scores, axis=3, keepdims=True)  70.2 us
    all_to_all x1, waiting for transfers between devices, on_device(): lax.all_to_all(head_view(queries), 'seq', split_axis=2, concat_axis=1, ti...  38 us
  transfers between devices with their start and end apart: 6, of which 6 were waited for; matrix products, arithmetic and copies ran while one was open for 5% of the time, Pallas kernels for 0%

profile of v1, /device:TPU:0, one launch (start us, length us, event | category | flops | bytes accessed | tf_op | source)
XLA Modules:
  0.0 1211.2 jit_solution(15570510702407797911)
XLA Ops:
  0.6 6.2 copy.85
  6.8 4.6 copy.86
  11.5 4.8 all-to-all-start
  16.3 6.2 copy.89
  22.5 4.6 copy.90
  27.2 38.0 %all-to-all-done = bf16[2,512,16,128]{1,3,0,2:T(8,128)(2,1)} async-done(((bf16[2,512,16,128]{1,3,0,2:T(8,128)(2,1)}), bf16[2,512,16,128]{1,3,0,2:T(8,128)(2,1)}, u32[]{:S(2)}, u32[]{:S(2)}) %all-to-all-start) | async-done | bytes 4194336 | tf_op jit(solution)/shard_map/all_to_all | solution.py:103
  65.2 4.8 all-to-all-start.1
  70.1 6.2 copy.93
  76.3 6.4 copy.94
  82.7 35.6 %all-to-all-done.1 = bf16[2,512,16,128]{1,3,0,2:T(8,128)(2,1)} async-done(((bf16[2,512,16,128]{1,3,0,2:T(8,128)(2,1)}), bf16[2,512,16,128]{1,3,0,2:T(8,128)(2,1)}, u32[]{:S(2)}, u32[]{:S(2)}) %all-to-all-start.1) | async-done | bytes 4194336 | tf_op jit(solution)/shard_map/all_to_all | solution.py:104
  118.3 4.8 all-to-all-start.2
  123.1 6.2 copy.97
  129.3 4.6 copy.98
  133.9 37.4 %all-to-all-done.2 = bf16[2,512,16,128]{3,1,0,2:T(8,128)(2,1)} async-done(((bf16[2,512,16,128]{3,1,0,2:T(8,128)(2,1)}), bf16[2,512,16,128]{3,1,0,2:T(8,128)(2,1)}, u32[]{:S(2)}, u32[]{:S(2)}) %all-to-all-start.2) | async-done | bytes 4194336 | tf_op jit(solution)/shard_map/all_to_all | solution.py:110
  171.3 4.9 all-to-all-start.3
  176.2 2.5 copy.96
  178.7 2.4 fusion.82
  181.1 5.3 collective-permute-start
  186.5 7.2 copy.88
  193.7 7.2 copy.92
  201.0 23.5 %all-to-all-done.3 = bf16[2,512,16,128]{1,3,0,2:T(8,128)(2,1)} async-done(((bf16[2,512,16,128]{1,3,0,2:T(8,128)(2,1)}), bf16[2,512,16,128]{1,3,0,2:T(8,128)(2,1)}, u32[]{:S(2)}, u32[]{:S(2)}) %all-to-all-start.3) | async-done | bytes 4194336 | tf_op jit(solution)/shard_map/all_to_all | solution.py:107
  224.4 7.3 copy.100
  232.3 1.5 fusion.74
  233.8 3.2 fusion.73
  237.0 615.2 %while.15 = (s32[]{:T(128)}, f32[2,2048,4,128]{1,3,2,0:T(8,128)}, f32[2,2048,4,128]{1,3,2,0:T(8,128)}, bf16[4,2,512,4,128]{4,2,0,3,1:T(8,128)(2,1)}, s32[4]{0:T(...) while((s32[]{:T(128)}, f32[2,2048,4,128]{1,3,2,0:T(8,128)}, ...), condition=%wide.region_4.5_spmd.clone, body=%wide.region_0.4_spmd.clone.sunk | while | flops 13069996032 | bytes 392267616 | solution.py:87
  251.4 0.6 dynamic_slice.50
  253.8 18.1 %fusion.118 = f32[2,4,512,2048]{3,2,1,0:T(8,128)} fusion(bf16[2,2048,4,128]{3,1,2,0:T(8,128)(2,1)} %get-tuple-element.207, bf16[2,2048,4,128]{3,1,2,0:T(8,128)(2,1)} %get-tuple-element.206, s32[]{:T(128)S(6)} %select_n.6), kind=kOutput, calls=%fused_computation.21.clone.1 | convolution fusion | flops 2147483648 | bytes 38797316 | tf_op jit(solution)/shard_map/while/body/eval_jaxpr/bqhd,bkhd->bhqk/dot_general | solution.py:72
  272.0 17.5 %fusion.119 = (f32[2,4,512]{2,1,0:T(4,128)S(1)}, f32[2,4,512,2048]{3,2,1,0:T(8,128)}) fusion(bf16[2,2048,4,128]{3,1,2,0:T(8,128)(2,1)} %get-tuple-element.205, bf16[2,2048,4,128]{3,1,2,0:T(8,128)(2,1)} %get-tuple-element.204, s32[]{:T(128)S(6)} %select_n.6), kind=kOutput, calls=%fused_computation.54.clone.1 | convolution fusion | flops 2172651520 | bytes 38813700 | tf_op jit(solution)/shard_map/while/body/eval_jaxpr/sub | solution.py:65
  289.5 45.7 %fusion.120 = bf16[4,2,512,4,128]{4,2,0,3,1:T(8,128)(2,1)} fusion(bf16[4,2,512,4,128]{4,2,0,3,1:T(8,128)(2,1)} %get-tuple-element.190, s32[]{:T(128)S(6)} %copy.120, bf16[2,2048,4,128]{3,1,2,0:T(8,128)(2,1)} %get-tuple-element.205, f32[2,4,512,2048]{3,2,1,0:T(8,128)} %fusion.118, f32[2,4,512,2048]{3,2,1,0:T(8,128)} %get-tuple-element.173, ...), kind=kOutput, calls=%fused_computation.19.clone.1 | convolution fusion | flops 2206734336 | bytes 139493376 | tf_op jit(solution)/shard_map/while/body/eval_jaxpr/bhqk,bkhd->bqhd/dot_general | solution.py:77
  335.2 46.5 %bitcast_add_fusion.4 = f32[2,2048,4,128]{1,3,2,0:T(8,128)} fusion(f32[2,2048,4,128]{1,3,2,0:T(8,128)} %get-tuple-element.188, f32[2,4,512,2048]{3,2,1,0:T(8,128)} %fusion.118, pred[]{:T(512)S(6)} %compare.3, bf16[2,2048,4,128]{3,1,2,0:T(8,128)(2,1)} %get-tuple-element.204, s32[]{:T(128)S(6)} %select_n.6, ...), kind=kOutput, calls=%fused_computation.16.clone.1 | convolution fusion | flops 2210404352 | bytes 152076288 | tf_op jit(solution)/shard_map/while/body/eval_jaxpr/bhqk,bqhd->bkhd/dot_general | solution.py:80
  381.7 17.1 %bitcast_add_fusion.5 = f32[2,2048,4,128]{1,3,2,0:T(8,128)} fusion(f32[2,2048,4,128]{1,3,2,0:T(8,128)} %get-tuple-element.189, pred[]{:T(512)S(6)} %compare.3, bf16[2,2048,4,128]{3,1,2,0:T(8,128)(2,1)} %get-tuple-element.206, s32[]{:T(128)S(6)} %select_n.6, f32[2,4,512]{2,1,0:T(4,128)S(1)} %get-tuple-element.174, ...), kind=kOutput, calls=%fused_computation.15.clone.1 | convolution fusion | flops 4332722176 | bytes 23086592 | tf_op jit(solution)/shard_map/while/body/eval_jaxpr/bhqk,bqhd->bkhd/dot_general | solution.py:69
  401.2 18.1 %fusion.118 = f32[2,4,512,2048]{3,2,1,0:T(8,128)} fusion(bf16[2,2048,4,128]{3,1,2,0:T(8,128)(2,1)} %get-tuple-element.207, bf16[2,2048,4,128]{3,1,2,0:T(8,128)(2,1)} %get-tuple-element.206, s32[]{:T(128)S(6)} %select_n.6), kind=kOutput, calls=%fused_computation.21.clone.1 | convolution fusion | flops 2147483648 | bytes 38797316 | tf_op jit(solution)/shard_map/while/body/eval_jaxpr/bqhd,bkhd->bhqk/dot_general | solution.py:72
  419.4 17.6 %fusion.119 = (f32[2,4,512]{2,1,0:T(4,128)S(1)}, f32[2,4,512,2048]{3,2,1,0:T(8,128)}) fusion(bf16[2,2048,4,128]{3,1,2,0:T(8,128)(2,1)} %get-tuple-element.205, bf16[2,2048,4,128]{3,1,2,0:T(8,128)(2,1)} %get-tuple-element.204, s32[]{:T(128)S(6)} %select_n.6), kind=kOutput, calls=%fused_computation.54.clone.1 | convolution fusion | flops 2172651520 | bytes 38813700 | tf_op jit(solution)/shard_map/while/body/eval_jaxpr/sub | solution.py:65
  436.9 45.7 %fusion.120 = bf16[4,2,512,4,128]{4,2,0,3,1:T(8,128)(2,1)} fusion(bf16[4,2,512,4,128]{4,2,0,3,1:T(8,128)(2,1)} %get-tuple-element.190, s32[]{:T(128)S(6)} %copy.120, bf16[2,2048,4,128]{3,1,2,0:T(8,128)(2,1)} %get-tuple-element.205, f32[2,4,512,2048]{3,2,1,0:T(8,128)} %fusion.118, f32[2,4,512,2048]{3,2,1,0:T(8,128)} %get-tuple-element.173, ...), kind=kOutput, calls=%fused_computation.19.clone.1 | convolution fusion | flops 2206734336 | bytes 139493376 | tf_op jit(solution)/shard_map/while/body/eval_jaxpr/bhqk,bkhd->bqhd/dot_general | solution.py:77
  482.6 48.8 %bitcast_add_fusion.4 = f32[2,2048,4,128]{1,3,2,0:T(8,128)} fusion(f32[2,2048,4,128]{1,3,2,0:T(8,128)} %get-tuple-element.188, f32[2,4,512,2048]{3,2,1,0:T(8,128)} %fusion.118, pred[]{:T(512)S(6)} %compare.3, bf16[2,2048,4,128]{3,1,2,0:T(8,128)(2,1)} %get-tuple-element.204, s32[]{:T(128)S(6)} %select_n.6, ...), kind=kOutput, calls=%fused_computation.16.clone.1 | convolution fusion | flops 2210404352 | bytes 152076288 | tf_op jit(solution)/shard_map/while/body/eval_jaxpr/bhqk,bqhd->bkhd/dot_general | solution.py:80
  531.5 18.3 %bitcast_add_fusion.5 = f32[2,2048,4,128]{1,3,2,0:T(8,128)} fusion(f32[2,2048,4,128]{1,3,2,0:T(8,128)} %get-tuple-element.189, pred[]{:T(512)S(6)} %compare.3, bf16[2,2048,4,128]{3,1,2,0:T(8,128)(2,1)} %get-tuple-element.206, s32[]{:T(128)S(6)} %select_n.6, f32[2,4,512]{2,1,0:T(4,128)S(1)} %get-tuple-element.174, ...), kind=kOutput, calls=%fused_computation.15.clone.1 | convolution fusion | flops 4332722176 | bytes 23086592 | tf_op jit(solution)/shard_map/while/body/eval_jaxpr/bhqk,bqhd->bkhd/dot_general | solution.py:69
  552.3 18.1 %fusion.118 = f32[2,4,512,2048]{3,2,1,0:T(8,128)} fusion(bf16[2,2048,4,128]{3,1,2,0:T(8,128)(2,1)} %get-tuple-element.207, bf16[2,2048,4,128]{3,1,2,0:T(8,128)(2,1)} %get-tuple-element.206, s32[]{:T(128)S(6)} %select_n.6), kind=kOutput, calls=%fused_computation.21.clone.1 | convolution fusion | flops 2147483648 | bytes 38797316 | tf_op jit(solution)/shard_map/while/body/eval_jaxpr/bqhd,bkhd->bhqk/dot_general | solution.py:72
  570.4 17.6 %fusion.119 = (f32[2,4,512]{2,1,0:T(4,128)S(1)}, f32[2,4,512,2048]{3,2,1,0:T(8,128)}) fusion(bf16[2,2048,4,128]{3,1,2,0:T(8,128)(2,1)} %get-tuple-element.205, bf16[2,2048,4,128]{3,1,2,0:T(8,128)(2,1)} %get-tuple-element.204, s32[]{:T(128)S(6)} %select_n.6), kind=kOutput, calls=%fused_computation.54.clone.1 | convolution fusion | flops 2172651520 | bytes 38813700 | tf_op jit(solution)/shard_map/while/body/eval_jaxpr/sub | solution.py:65
  587.9 45.7 %fusion.120 = bf16[4,2,512,4,128]{4,2,0,3,1:T(8,128)(2,1)} fusion(bf16[4,2,512,4,128]{4,2,0,3,1:T(8,128)(2,1)} %get-tuple-element.190, s32[]{:T(128)S(6)} %copy.120, bf16[2,2048,4,128]{3,1,2,0:T(8,128)(2,1)} %get-tuple-element.205, f32[2,4,512,2048]{3,2,1,0:T(8,128)} %fusion.118, f32[2,4,512,2048]{3,2,1,0:T(8,128)} %get-tuple-element.173, ...), kind=kOutput, calls=%fused_computation.19.clone.1 | convolution fusion | flops 2206734336 | bytes 139493376 | tf_op jit(solution)/shard_map/while/body/eval_jaxpr/bhqk,bkhd->bqhd/dot_general | solution.py:77
  633.7 48.8 %bitcast_add_fusion.4 = f32[2,2048,4,128]{1,3,2,0:T(8,128)} fusion(f32[2,2048,4,128]{1,3,2,0:T(8,128)} %get-tuple-element.188, f32[2,4,512,2048]{3,2,1,0:T(8,128)} %fusion.118, pred[]{:T(512)S(6)} %compare.3, bf16[2,2048,4,128]{3,1,2,0:T(8,128)(2,1)} %get-tuple-element.204, s32[]{:T(128)S(6)} %select_n.6, ...), kind=kOutput, calls=%fused_computation.16.clone.1 | convolution fusion | flops 2210404352 | bytes 152076288 | tf_op jit(solution)/shard_map/while/body/eval_jaxpr/bhqk,bqhd->bkhd/dot_general | solution.py:80
  682.5 18.3 %bitcast_add_fusion.5 = f32[2,2048,4,128]{1,3,2,0:T(8,128)} fusion(f32[2,2048,4,128]{1,3,2,0:T(8,128)} %get-tuple-element.189, pred[]{:T(512)S(6)} %compare.3, bf16[2,2048,4,128]{3,1,2,0:T(8,128)(2,1)} %get-tuple-element.206, s32[]{:T(128)S(6)} %select_n.6, f32[2,4,512]{2,1,0:T(4,128)S(1)} %get-tuple-element.174, ...), kind=kOutput, calls=%fused_computation.15.clone.1 | convolution fusion | flops 4332722176 | bytes 23086592 | tf_op jit(solution)/shard_map/while/body/eval_jaxpr/bhqk,bqhd->bkhd/dot_general | solution.py:69
  703.3 18.1 %fusion.118 = f32[2,4,512,2048]{3,2,1,0:T(8,128)} fusion(bf16[2,2048,4,128]{3,1,2,0:T(8,128)(2,1)} %get-tuple-element.207, bf16[2,2048,4,128]{3,1,2,0:T(8,128)(2,1)} %get-tuple-element.206, s32[]{:T(128)S(6)} %select_n.6), kind=kOutput, calls=%fused_computation.21.clone.1 | convolution fusion | flops 2147483648 | bytes 38797316 | tf_op jit(solution)/shard_map/while/body/eval_jaxpr/bqhd,bkhd->bhqk/dot_general | solution.py:72
  721.4 17.5 %fusion.119 = (f32[2,4,512]{2,1,0:T(4,128)S(1)}, f32[2,4,512,2048]{3,2,1,0:T(8,128)}) fusion(bf16[2,2048,4,128]{3,1,2,0:T(8,128)(2,1)} %get-tuple-element.205, bf16[2,2048,4,128]{3,1,2,0:T(8,128)(2,1)} %get-tuple-element.204, s32[]{:T(128)S(6)} %select_n.6), kind=kOutput, calls=%fused_computation.54.clone.1 | convolution fusion | flops 2172651520 | bytes 38813700 | tf_op jit(solution)/shard_map/while/body/eval_jaxpr/sub | solution.py:65
  739.0 45.7 %fusion.120 = bf16[4,2,512,4,128]{4,2,0,3,1:T(8,128)(2,1)} fusion(bf16[4,2,512,4,128]{4,2,0,3,1:T(8,128)(2,1)} %get-tuple-element.190, s32[]{:T(128)S(6)} %copy.120, bf16[2,2048,4,128]{3,1,2,0:T(8,128)(2,1)} %get-tuple-element.205, f32[2,4,512,2048]{3,2,1,0:T(8,128)} %fusion.118, f32[2,4,512,2048]{3,2,1,0:T(8,128)} %get-tuple-element.173, ...), kind=kOutput, calls=%fused_computation.19.clone.1 | convolution fusion | flops 2206734336 | bytes 139493376 | tf_op jit(solution)/shard_map/while/body/eval_jaxpr/bhqk,bkhd->bqhd/dot_general | solution.py:77
  784.7 48.8 %bitcast_add_fusion.4 = f32[2,2048,4,128]{1,3,2,0:T(8,128)} fusion(f32[2,2048,4,128]{1,3,2,0:T(8,128)} %get-tuple-element.188, f32[2,4,512,2048]{3,2,1,0:T(8,128)} %fusion.118, pred[]{:T(512)S(6)} %compare.3, bf16[2,2048,4,128]{3,1,2,0:T(8,128)(2,1)} %get-tuple-element.204, s32[]{:T(128)S(6)} %select_n.6, ...), kind=kOutput, calls=%fused_computation.16.clone.1 | convolution fusion | flops 2210404352 | bytes 152076288 | tf_op jit(solution)/shard_map/while/body/eval_jaxpr/bhqk,bqhd->bkhd/dot_general | solution.py:80
  833.5 18.3 %bitcast_add_fusion.5 = f32[2,2048,4,128]{1,3,2,0:T(8,128)} fusion(f32[2,2048,4,128]{1,3,2,0:T(8,128)} %get-tuple-element.189, pred[]{:T(512)S(6)} %compare.3, bf16[2,2048,4,128]{3,1,2,0:T(8,128)(2,1)} %get-tuple-element.206, s32[]{:T(128)S(6)} %select_n.6, f32[2,4,512]{2,1,0:T(4,128)S(1)} %get-tuple-element.174, ...), kind=kOutput, calls=%fused_computation.15.clone.1 | convolution fusion | flops 4332722176 | bytes 23086592 | tf_op jit(solution)/shard_map/while/body/eval_jaxpr/bhqk,bqhd->bkhd/dot_general | solution.py:69
  852.2 7.1 copy.102
  859.4 7.1 copy.103
  866.5 6.4 pad_maximum_fusion.1
  872.9 4.0 fusion.81
  876.9 0.7 fusion.72
  877.6 1.8 collective-permute-start.1
  879.4 138.7 %collective-permute-done.1 = bf16[3,2,32,32,4,128]{5,3,2,4,1,0:T(8,128)(2,1)S(1)} collective-permute-done((bf16[3,2,32,32,4,128]{5,3,2,4,1,0:T(8,128)(2,1)S(1)}, bf16[3,2,32,32,4,128]{5,3,2,4,1,0:T(8,128)(2,1)S(1)}, u32[]{:S(2)}, u32[]{:S(2)}) %collective-permute-start.1) | collective-permute-done | bytes 6291488 | tf_op jit(solution)/shard_map/ppermute | solution.py:27
  1018.1 1.6 fusion.71
  1019.7 1.3 slice_bitcast_fusion.3
  1021.0 1.7 pad_maximum_fusion.2
  1022.6 141.1 %all_to_all.74 = bf16[4,3,2,512,4,128]{5,3,4,2,1,0:T(8,128)(2,1)S(1)} all-to-all(bf16[4,3,2,512,4,128]{5,3,4,2,1,0:T(8,128)(2,1)S(1)} %pad_maximum_fusion.2), channel_id=1, replica_groups=mesh['win'=8,'seq'=4] {'seq'}, dimensions={0} | all-to-all | bytes 25165824 | tf_op jit(solution)/shard_map/all_to_all | solution.py:14
  1163.8 4.0 fusion.80
  1167.8 5.2 copy.106
  1173.0 7.8 squeeze.15
  1180.8 7.4 copy.105
  1188.1 7.8 squeeze.14
  1195.9 7.4 copy.104
  1203.3 7.8 squeeze.13
  (24 shorter events, 2.5 us)
Async XLA Ops:
  11.5 53.7 %all-to-all-start = ((bf16[2,512,16,128]{1,3,0,2:T(8,128)(2,1)}), bf16[2,512,16,128]{1,3,0,2:T(8,128)(2,1)}, u32[]{:S(2)}, u32[]{:S(2)}) async-start(bf16[2,512,16,128]{1,3,0,2:T(8,128)(2,1)} %copy.86), calls=%async_computation | async-start | bytes 8388608 | tf_op jit(solution)/shard_map/all_to_all | solution.py:103
  65.2 53.0 %all-to-all-start.1 = ((bf16[2,512,16,128]{1,3,0,2:T(8,128)(2,1)}), bf16[2,512,16,128]{1,3,0,2:T(8,128)(2,1)}, u32[]{:S(2)}, u32[]{:S(2)}) async-start(bf16[2,512,16,128]{1,3,0,2:T(8,128)(2,1)} %copy.90), calls=%async_computation.1 | async-start | bytes 8388608 | tf_op jit(solution)/shard_map/all_to_all | solution.py:104
  118.3 53.0 %all-to-all-start.2 = ((bf16[2,512,16,128]{3,1,0,2:T(8,128)(2,1)}), bf16[2,512,16,128]{3,1,0,2:T(8,128)(2,1)}, u32[]{:S(2)}, u32[]{:S(2)}) async-start(bf16[2,512,16,128]{3,1,0,2:T(8,128)(2,1)} %copy.94), calls=%async_computation.2 | async-start | bytes 8388608 | tf_op jit(solution)/shard_map/all_to_all | solution.py:110
  171.3 53.1 %all-to-all-start.3 = ((bf16[2,512,16,128]{1,3,0,2:T(8,128)(2,1)}), bf16[2,512,16,128]{1,3,0,2:T(8,128)(2,1)}, u32[]{:S(2)}, u32[]{:S(2)}) async-start(bf16[2,512,16,128]{1,3,0,2:T(8,128)(2,1)} %copy.98), calls=%async_computation.3 | async-start | bytes 8388608 | tf_op jit(solution)/shard_map/all_to_all | solution.py:107
  181.1 51.2 %collective-permute-start = (bf16[2,32,32,4,128]{4,2,1,3,0:T(8,128)(2,1)}, bf16[2,32,32,4,128]{4,2,1,3,0:T(8,128)(2,1)}, u32[]{:S(2)}, u32[]{:S(2)}) collective-permute-start(bf16[2,32,32,4,128]{4,2,1,3,0:T(8,128)(2,1)} %get-tuple-element.115), channel_id=1, source_target_pairs={{4,0},{8,4},{12,8},{16,12},{20,16},{24,20},{28,24},{0,28},{5,1},{9... | collective-permute-start | bytes 6291464 | tf_op jit(solution)/shard_map/ppermute | solution.py:27
  251.4 20.6 %copy-start = (s32[4]{0:T(128)}, s32[4]{0:T(128)S(1)}, u32[]{:S(2)}) copy-start(s32[4]{0:T(128)S(1)} %get-tuple-element.203) | copy-start | bytes 52 | tf_op jit(solution)/shard_map/while
  381.7 17.1 %copy-start.1 = (s32[4]{0:T(128)S(1)}, s32[4]{0:T(128)}, u32[]{:S(2)}) copy-start(s32[4]{0:T(128)} %copy-done) | copy-start | bytes 52 | tf_op jit(solution)/shard_map/while
  398.8 20.6 %copy-start = (s32[4]{0:T(128)}, s32[4]{0:T(128)S(1)}, u32[]{:S(2)}) copy-start(s32[4]{0:T(128)S(1)} %get-tuple-element.203) | copy-start | bytes 52 | tf_op jit(solution)/shard_map/while
  531.5 18.3 %copy-start.1 = (s32[4]{0:T(128)S(1)}, s32[4]{0:T(128)}, u32[]{:S(2)}) copy-start(s32[4]{0:T(128)} %copy-done) | copy-start | bytes 52 | tf_op jit(solution)/shard_map/while
  549.8 20.6 %copy-start = (s32[4]{0:T(128)}, s32[4]{0:T(128)S(1)}, u32[]{:S(2)}) copy-start(s32[4]{0:T(128)S(1)} %get-tuple-element.203) | copy-start | bytes 52 | tf_op jit(solution)/shard_map/while
  682.5 18.3 %copy-start.1 = (s32[4]{0:T(128)S(1)}, s32[4]{0:T(128)}, u32[]{:S(2)}) copy-start(s32[4]{0:T(128)} %copy-done) | copy-start | bytes 52 | tf_op jit(solution)/shard_map/while
  700.8 20.6 %copy-start = (s32[4]{0:T(128)}, s32[4]{0:T(128)S(1)}, u32[]{:S(2)}) copy-start(s32[4]{0:T(128)S(1)} %get-tuple-element.203) | copy-start | bytes 52 | tf_op jit(solution)/shard_map/while
  833.5 18.3 %copy-start.1 = (s32[4]{0:T(128)S(1)}, s32[4]{0:T(128)}, u32[]{:S(2)}) copy-start(s32[4]{0:T(128)} %copy-done) | copy-start | bytes 52 | tf_op jit(solution)/shard_map/while
  877.6 140.5 %collective-permute-start.1 = (bf16[3,2,32,32,4,128]{5,3,2,4,1,0:T(8,128)(2,1)S(1)}, bf16[3,2,32,32,4,128]{5,3,2,4,1,0:T(8,128)(2,1)S(1)}, u32[]{:S(2)}, u32[]{:S(2)}) collective-permute-start(bf16[3,2,32,32,4,128]{5,3,2,4,1,0:T(8,128)(2,1)S(1)} %fusion.72), channel_id=1, source_target_pairs={{28,0},{0,4},{4,8},{8,12},{12,16},{16,20},{20,24},{24,28},{29,1},{... | collective-permute-start | bytes 18874376 | tf_op jit(solution)/shard_map/ppermute | solution.py:27
